TPU v7x, 32 devices: a whole 2x2x4 slice. The times are simulated.
32 devices in a mesh: dp: 4 (over z), mp: 8 (over y, x, core).
Axes of the slice: x: 2, y: 2, z: 4, core: 2. Of those that a mesh axis runs over, the one named last changes fastest.
Arguments:
- gate_pre: bfloat16 [768, 14336], P('dp', 'mp'), may hold values from -8 to 8
- up_pre: bfloat16 [768, 14336], P('dp', 'mp'), may hold values from -6 to 6
- d_out: bfloat16 [768, 4096], P(('dp', 'mp')), may hold values from -6 to 6
- down_weight: bfloat16 [4096, 14336], P('dp', 'mp'), may hold values from -0.046875 to 0.046875
Outputs:
- d_gate: bfloat16 [768, 14336], P('dp', 'mp')
- d_up: bfloat16 [768, 14336], P('dp', 'mp')
- grad_down: bfloat16 [4096, 14336], P('dp', 'mp')
All inputs are finite; a program needn't handle non-finite values.
Results may differ from a plain program's by a relative error of at most 0.0095.
Values may be sent and summed in bfloat16 or wider, within the bound.
A program may use at most 128 MiB of HBM per device.

v0:
```python
import jax
import jax.numpy as jnp
from jax import lax
from jax.sharding import PartitionSpec as P


def body(gate_pre, up_pre, d_out, down_weight):
    gate = gate_pre.astype(jnp.float32)
    upper = up_pre.astype(jnp.float32)
    sig = jax.nn.sigmoid(gate)
    act = gate * sig
    hidden = (act * upper).astype(jnp.bfloat16)
    replicas = lax.axis_size("dp")
    full_out = lax.all_gather(d_out, "mp", axis=0, tiled=True)
    tok_rows = full_out.shape[0]
    local_hidden = hidden.shape[1]
    columns = full_out
    d_hidden = jnp.dot(
        columns,
        lax.all_gather(down_weight, "dp", axis=0, tiled=True),
        preferred_element_type=jnp.float32,
    )
    d_up = (d_hidden * act).astype(jnp.bfloat16)
    d_gate = (d_hidden * upper * sig * (1.0 + gate * (1.0 - sig))).astype(jnp.bfloat16)
    feature_rows = down_weight.shape[0]
    moved = lax.all_to_all(full_out, "dp", split_axis=1, concat_axis=0, tiled=True)
    piece = lax.all_gather(hidden, "dp", axis=0, tiled=True)
    blocks = piece.shape[0] // tok_rows
    columns = moved
    terms = jnp.einsum(
        "rtd,rtf->rdf",
        columns.reshape(blocks, tok_rows, feature_rows),
        piece.reshape(blocks, tok_rows, local_hidden),
        preferred_element_type=jnp.float32,
    )
    total = jnp.sum(terms.astype(jnp.bfloat16).astype(jnp.float32), axis=0)
    grad_down = (total / replicas).astype(jnp.bfloat16)
    return (d_gate, d_up, grad_down)


def solution(mesh):
    in_specs = (P("dp", "mp"), P("dp", "mp"), P(("dp", "mp"), None), P("dp", "mp"))
    out_specs = (P("dp", "mp"), P("dp", "mp"), P("dp", "mp"))
    return jax.shard_map(body, mesh=mesh, in_specs=in_specs, out_specs=out_specs, check_vma=False)
```

profile of v0, /device:TPU:0, one launch (start us, length us, event | category | flops | bytes accessed | tf_op | source)
XLA Modules:
  0.0 415.6 jit_solution(11324991727766426773)
XLA Ops:
  7.2 0.0 all-gather.4.cloned.1.call-start
  7.2 0.7 all-gather.4.cloned.1.call-update
  7.9 0.0 copy-start.1
  7.9 0.0 copy-start.2
  7.9 0.0 all-gather.6.cloned.1.call-start
  8.0 0.7 all-gather.6.cloned.1.call-update
  8.7 0.0 all-gather.8.cloned.1.call-start
  8.7 29.6 %all-gather.4.cloned.1.call-done = bf16[192,4096]{1,0:T(8,128)(2,1)} async-done(((bf16[24,4096]{1,0:T(8,128)(2,1)}), bf16[192,4096]{1,0:T(8,128)(2,1)}) %all-gather.4.cloned.1.call-update) | async-done | bytes 1572880 | tf_op jit(solution)/shard_map/all_gather | solution.py:14
  38.3 254.1 %all-gather.6.cloned.1.call-done = bf16[4096,1792]{1,0:T(8,128)(2,1)} async-done(((bf16[1024,1792]{1,0:T(8,128)(2,1)}), bf16[4096,1792]{1,0:T(8,128)(2,1)}) %all-gather.6.cloned.1.call-update) | async-done | bytes 14680080 | tf_op jit(solution)/shard_map/all_gather | solution.py:20
  292.4 0.0 copy-done.1
  292.4 0.0 copy-done.2
  292.4 0.0 copy-start
  292.4 10.4 %multiply_convert_fusion.1 = (bf16[192,1792]{1,0:T(8,128)(2,1)}, bf16[192,1792]{1,0:T(8,128)(2,1)}, bf16[192,1792]{1,0:T(8,128)(2,1)}) fusion(bf16[192,1792]{1,0:T(8,128)(2,1)S(1)} %copy-done.1, bf16[192,1792]{1,0:T(8,128)(2,1)S(1)} %copy-done.2, bf16[192,4096]{1,0:T(8,128)(2,1)} %all-gather.4.cloned.1.call-done, ...), kind=kOutput, calls=%fused_computation.18 | convolution fusion | flops 2824421376 | bytes 19693568 | tf_op jit(solution)/shard_map/dot_general | solution.py:18
  302.8 0.0 all-gather.8.cloned.1.call-update
  302.8 0.0 copy-done
  302.8 0.1 copy.12
  303.0 77.7 %all_to_all.16 = bf16[192,4,1024]{2,0,1:T(8,128)(2,1)S(1)} all-to-all(bf16[192,4,1024]{2,0,1:T(8,128)(2,1)S(1)} %bitcast.13), channel_id=1, replica_groups=mesh['dp'=4,'mp'=8] {'dp'}, dimensions={1} | all-to-all | bytes 3145728 | tf_op jit(solution)/shard_map/all_to_all | solution.py:26
  380.6 6.8 %all-gather.8.cloned.1.call-done = bf16[768,1792]{1,0:T(8,128)(2,1)} async-done(((bf16[192,1792]{1,0:T(8,128)(2,1)}), bf16[768,1792]{1,0:T(8,128)(2,1)}) %all-gather.8.cloned.1.call-update) | async-done | bytes 2752528 | tf_op jit(solution)/shard_map/all_gather | solution.py:27
  387.5 9.6 %convert_reduce_fusion = f32[1792,1024]{1,0:T(8,128)} fusion(bf16[4,192,1792]{2,1,0:T(8,128)(2,1)} %bitcast.15, bf16[192,4,1024]{2,0,1:T(8,128)(2,1)S(1)} %all_to_all.16), kind=kOutput, calls=%fused_computation | convolution fusion | flops 2838757376 | bytes 11665408 | tf_op jit(solution)/shard_map/rtd,rtf->rdf/dot_general | solution.py:30
  397.0 6.1 %fusion = bf16[1024,1792]{0,1:T(8,128)(2,1)} fusion(f32[1792,1024]{1,0:T(8,128)} %convert_reduce_fusion), kind=kLoop, calls=%fused_computation.2 | loop fusion | flops 3670016 | bytes 11010048 | tf_op jit(solution)/shard_map/convert_element_type | solution.py:37
  403.1 5.9 %copy.9 = bf16[1024,1792]{1,0:T(8,128)(2,1)} copy(bf16[1024,1792]{0,1:T(8,128)(2,1)} %fusion) | data formatting | bytes 7340032
Async XLA Ops:
  7.2 31.1 %all-gather.4.cloned.1.call-start = ((), (), s32[]{:S(2)}) async-start(), calls=%async_computation.1 | async-start | bytes 1769472 | tf_op jit(solution)/shard_map/all_gather | solution.py:14
  7.9 284.5 %copy-start.1 = (bf16[192,1792]{1,0:T(8,128)(2,1)S(1)}, bf16[192,1792]{1,0:T(8,128)(2,1)}, u32[]{:S(2)}) copy-start(bf16[192,1792]{1,0:T(8,128)(2,1)} %param.4) | copy-start | bytes 2064388
  7.9 284.5 %copy-start.2 = (bf16[192,1792]{1,0:T(8,128)(2,1)S(1)}, bf16[192,1792]{1,0:T(8,128)(2,1)}, u32[]{:S(2)}) copy-start(bf16[192,1792]{1,0:T(8,128)(2,1)} %param.5) | copy-start | bytes 2064388
  7.9 284.5 %all-gather.6.cloned.1.call-start = ((), (), s32[]{:S(2)}) async-start(), calls=%async_computation.2 | async-start | bytes 18350080 | tf_op jit(solution)/shard_map/all_gather | solution.py:20
  8.7 378.8 %all-gather.8.cloned.1.call-start = ((), (), s32[]{:S(2)}) async-start(), calls=%async_computation.3 | async-start | bytes 3440640 | tf_op jit(solution)/shard_map/all_gather | solution.py:27
  292.4 10.4 %copy-start = (bf16[192,4096]{1,0:T(8,128)(2,1)S(1)}, bf16[192,4096]{1,0:T(8,128)(2,1)}, u32[]{:S(2)}) copy-start(bf16[192,4096]{1,0:T(8,128)(2,1)} %all-gather.4.cloned.1.call-done) | copy-start | bytes 4718596
Sparse Core Ops, SparseCore 0:
  9.9 28.3 all-gather.3
  39.9 252.4 all-gather.5
  302.9 84.5 all-gather.7
where the time goes:
time: 416 us
  waiting for transfers between devices  292 us (70%)
  blocking collectives  77.7 us (19%)
  matrix products  19.9 us (5%)
  between operations  13.8 us (3%)
  other arithmetic  6.09 us (1%)
  local copies, waits for them, and re-layouts  6.06 us (1%)
    all_gather x1, waiting for transfers between devices, body(): lax.all_gather(down_weight, 'dp', axis=0, tiled=True)  254 us
    all_to_all x1, blocking collectives, body(): lax.all_to_all(full_out, 'dp', split_axis=1, concat_axis=0, tiled=True)  77.7 us
    all_gather x1, waiting for transfers between devices, body(): full_out = lax.all_gather(d_out, 'mp', axis=0, tiled=True)  29.6 us
    dot_general x1, matrix products, body(): jnp.dot(columns, lax.all_gather(down_weight, 'dp', axis=0, tiled=True), p...  10.4 us
    dot_general x1, matrix products, body(): jnp.einsum('rtd,rtf->rdf', columns.reshape(blocks, tok_rows, feature_rows...  9.56 us
  transfers between devices with their start and end apart: 3, of which 3 were waited for; matrix products, arithmetic and copies ran while one was open for 0% of the time, Pallas kernels for 0%

commit v1 on v0

v1 whole, which is shorter than its diff:
```python
import functools

import jax
import jax.numpy as jnp
from jax import lax
from jax.experimental import pallas as pl
from jax.experimental.pallas import tpu as pltpu
from jax.sharding import PartitionSpec as P

MESH = pl.DeviceIdType.MESH


def plain(gate_pre, up_pre, d_out, down_weight):
    replicas, peers = lax.axis_size("dp"), lax.axis_size("mp")
    rows, features = d_out.shape[0], down_weight.shape[0]
    gate = gate_pre.astype(jnp.float32)
    upper = up_pre.astype(jnp.float32)
    sig = jax.nn.sigmoid(gate)
    act = gate * sig
    hidden = (act * upper).astype(jnp.bfloat16)
    columns = lax.all_to_all(d_out, "dp", split_axis=1, concat_axis=0, tiled=True)
    columns = lax.all_gather(columns.reshape(replicas, rows, features), "mp", axis=1)
    columns = columns.reshape(replicas * peers * rows, features)
    every_hidden = lax.all_gather(hidden, "dp", axis=0, tiled=True)
    share = jnp.dot(columns, down_weight, preferred_element_type=jnp.float32)
    d_hidden = lax.psum_scatter(share, "dp", scatter_dimension=0, tiled=True)
    d_up = (d_hidden * act).astype(jnp.bfloat16)
    d_gate = (d_hidden * upper * sig * (1.0 + gate * (1.0 - sig))).astype(jnp.bfloat16)
    total = lax.dot_general(
        columns, every_hidden, (((0,), (0,)), ((), ())), preferred_element_type=jnp.float32
    )
    return d_gate, d_up, (total / replicas).astype(jnp.bfloat16)


def solution(mesh):
    in_specs = (P("dp", "mp"), P("dp", "mp"), P(("dp", "mp"), None), P("dp", "mp"))
    out_specs = (P("dp", "mp"), P("dp", "mp"), P("dp", "mp"))
    return jax.shard_map(plain, mesh=mesh, in_specs=in_specs, out_specs=out_specs, check_vma=False)
```

time: 416 us -> 235 us (0.56)
  waiting for transfers between devices: 292 us -> 181 us
  blocking collectives: 77.7 us -> 13.6 us
  matrix products: 19.9 us -> 13.3 us
    all_gather x3 -> x2, waiting for transfers between devices: 291 us -> 82.6 us  [the longest x1 57.7 us: plain(): every_hidden = lax.all_gather(hidden, 'dp', axis=0, tiled=True)]
    reduce_scatter x0 -> x1, waiting for transfers between devices: none -> 98.1 us  [plain(): d_hidden = lax.psum_scatter(share, 'dp', scatter_dimension=0, tiled=True)]
    all_to_all x1, blocking collectives: 77.7 us -> 13.6 us  [plain(): lax.all_to_all(d_out, 'dp', split_axis=1, concat_axis=0, tiled=True)]
    dot_general x2, matrix products: 19.9 us -> 13.3 us  [the longest x1 6.85 us: plain(): share = jnp.dot(columns, down_weight, preferred_element_type=jnp.float32)]
where the time goes in v1:
time: 235 us; the launch traced here: 234 us
  waiting for transfers between devices  181 us (77%)
  between operations  13.8 us (6%)
  blocking collectives  13.6 us (6%)
  matrix products  13.3 us (6%)
  local copies, waits for them, and re-layouts  9.56 us (4%)
  other arithmetic  3.29 us (1%)
    reduce_scatter x1, waiting for transfers between devices, plain(): d_hidden = lax.psum_scatter(share, 'dp', scatter_dimension=0, tiled=True)  98.1 us
    all_gather x1, waiting for transfers between devices, plain(): every_hidden = lax.all_gather(hidden, 'dp', axis=0, tiled=True)  57.7 us
    all_gather x1, waiting for transfers between devices, plain(): lax.all_gather(columns.reshape(replicas, rows, features), 'mp', axis=1)  24.9 us
    all_to_all x1, blocking collectives, plain(): lax.all_to_all(d_out, 'dp', split_axis=1, concat_axis=0, tiled=True)  13.6 us
    dot_general x1, matrix products, plain(): share = jnp.dot(columns, down_weight, preferred_element_type=jnp.float32)  6.85 us
    dot_general x1, matrix products, plain(): lax.dot_general(columns, every_hidden, (((0,), (0,)), ((), ())), preferre...  6.42 us
    unnamed x5, local copies, waits for them, and re-layouts  5.92 us
  transfers between devices with their start and end apart: 3, of which 3 were waited for; matrix products, arithmetic and copies ran while one was open for 0% of the time, Pallas kernels for 0%

profile of v1, /device:TPU:0, one launch (start us, length us, event | category | flops | bytes accessed | tf_op | source)
XLA Modules:
  0.0 234.3 jit_solution(16648494803660841994)
XLA Ops:
  7.2 0.0 all-gather.6.cloned.1.call-start
  7.2 0.9 copy.17
  8.2 13.6 %all_to_all.16 = bf16[24,4,1024]{2,0,1:T(8,128)(2,1)S(1)} all-to-all(bf16[24,4,1024]{2,0,1:T(8,128)(2,1)S(1)} %bitcast.15), channel_id=1, replica_groups=mesh['dp'=4,'mp'=8] {'dp'}, dimensions={1} | all-to-all | bytes 393216 | tf_op jit(solution)/shard_map/all_to_all | solution.py:21
  21.8 0.8 copy.12
  22.6 0.0 all-gather.6.cloned.1.call-update
  22.6 0.0 reduce-scatter.2.cloned.1.call-start
  22.7 24.9 %all-gather.6.cloned.1.call-done = bf16[4,192,1024]{2,0,1:T(4,128)(2,1)} async-done(((bf16[4,24,1024]{2,0,1:T(4,128)(2,1)}), bf16[4,192,1024]{2,0,1:T(4,128)(2,1)}) %all-gather.6.cloned.1.call-update) | async-done | bytes 1572880 | tf_op jit(solution)/shard_map/all_gather | solution.py:22
  47.6 1.9 copy.13
  49.4 6.8 %fusion.9 = f32[768,1792]{1,0:T(8,128)} fusion(bf16[768,1024]{1,0:T(8,128)(2,1)S(1)} %bitcast.12, bf16[1024,1792]{1,0:T(8,128)(2,1)} %param.7), kind=kOutput, calls=%fused_computation.17 | convolution fusion | flops 2818572288 | bytes 10747904 | tf_op jit(solution)/shard_map/dot_general | solution.py:25
  56.3 0.0 copy-start
  56.3 0.0 copy-start.1
  56.3 0.0 reduce-scatter.2.cloned.1.call-update
  56.3 0.0 all-gather.4.cloned.1.call-start
  56.4 98.1 %reduce-scatter.2.cloned.1.call-done = f32[192,1792]{1,0:T(8,128)} async-done(((f32[768,1792]{1,0:T(8,128)}), f32[192,1792]{1,0:T(8,128)}) %reduce-scatter.2.cloned.1.call-update) | async-done | bytes 1376272 | tf_op jit(solution)/shard_map/reduce_scatter | solution.py:26
  154.5 0.0 copy-done
  154.5 0.0 copy-done.1
  154.5 3.3 %multiply_convert_fusion.1 = (bf16[192,1792]{1,0:T(8,128)(2,1)}, bf16[192,1792]{1,0:T(8,128)(2,1)}, bf16[192,1792]{1,0:T(8,128)(2,1)}) fusion(f32[192,1792]{1,0:T(8,128)} %reduce-scatter.2.cloned.1.call-done, bf16[192,1792]{1,0:T(8,128)(2,1)S(1)} %copy-done, bf16[192,1792]{1,0:T(8,128)(2,1)S(1)} %copy-done.1), kind=kLoop, calls=%fused_computation.15 | loop fusion | flops 5849088 | bytes 4816896 | tf_op jit(solution)/shard_map/convert_element_type | solution.py:27
  157.8 0.0 all-gather.4.cloned.1.call-update
  157.8 57.7 %all-gather.4.cloned.1.call-done = bf16[768,1792]{1,0:T(8,128)(2,1)} async-done(((bf16[192,1792]{1,0:T(8,128)(2,1)}), bf16[768,1792]{1,0:T(8,128)(2,1)}) %all-gather.4.cloned.1.call-update) | async-done | bytes 2752528 | tf_op jit(solution)/shard_map/all_gather | solution.py:24
  215.4 6.4 %fusion = bf16[1024,1792]{0,1:T(8,128)(2,1)} fusion(bf16[768,1792]{1,0:T(8,128)(2,1)} %all-gather.4.cloned.1.call-done, bf16[768,1024]{1,0:T(8,128)(2,1)S(1)} %bitcast.13), kind=kOutput, calls=%fused_computation.1 | convolution fusion | flops 2822242304 | bytes 7995392 | tf_op jit(solution)/shard_map/dot_general | solution.py:29
  221.9 5.9 %copy.14 = bf16[1024,1792]{1,0:T(8,128)(2,1)} copy(bf16[1024,1792]{0,1:T(8,128)(2,1)} %fusion) | data formatting | bytes 7340032
Async XLA Ops:
  7.2 40.4 %all-gather.6.cloned.1.call-start = ((), (), s32[]{:S(2)}) async-start(), calls=%async_computation.4 | async-start | bytes 1769472 | tf_op jit(solution)/shard_map/all_gather | solution.py:22
  22.6 131.9 %reduce-scatter.2.cloned.1.call-start = ((), (), s32[]{:S(2)}) async-start(), calls=%async_computation.2 | async-start | bytes 6881280 | tf_op jit(solution)/shard_map/reduce_scatter | solution.py:26
  56.3 98.2 %copy-start = (bf16[192,1792]{1,0:T(8,128)(2,1)S(1)}, bf16[192,1792]{1,0:T(8,128)(2,1)}, u32[]{:S(2)}) copy-start(bf16[192,1792]{1,0:T(8,128)(2,1)} %param.4) | copy-start | bytes 2064388
  56.3 98.2 %copy-start.1 = (bf16[192,1792]{1,0:T(8,128)(2,1)S(1)}, bf16[192,1792]{1,0:T(8,128)(2,1)}, u32[]{:S(2)}) copy-start(bf16[192,1792]{1,0:T(8,128)(2,1)} %param.5) | copy-start | bytes 2064388
  56.3 159.1 %all-gather.4.cloned.1.call-start = ((), (), s32[]{:S(2)}) async-start(), calls=%async_computation.3 | async-start | bytes 3440640 | tf_op jit(solution)/shard_map/all_gather | solution.py:24
Sparse Core Ops, SparseCore 0:
  22.7 24.7 all-gather.5
  56.4 97.9 reduce-scatter.1
  157.9 57.5 all-gather.3
